TPU v7x, 256 devices: a whole 4x4x8 slice. The times are simulated.
256 devices in a mesh: gx: 8 (over z_lo, y), gy: 8 (over x, core), dir: 4 (over z_hi).
Axes of the slice: x: 4, y: 4, z: 8 (z_hi: 4, z_lo: 2; z = z_hi * 2 + z_lo), core: 2. Of those that a mesh axis runs over, the one named last changes fastest.
Arguments:
- directions: float32 [32, 1024, 2048], P('dir', 'gx', 'gy'), may hold values from -6 to 6
- velocity: float32 [2, 1024, 2048], P(None, 'gx', 'gy'), may hold values from -6 to 6
- viscosity: float32 [1024, 2048], P('gx', 'gy'), may hold values from 0.5 to 2
- basal_drag: float32 [1024, 2048], P('gx', 'gy'), may hold values from 0.5 to 8
- misfit_weight: float32 [1024, 2048], P('gx', 'gy'), may hold values from 1 to 10
- ice_mask: int32 [1024, 2048], P('gx', 'gy'), may hold values 0 or 1
- grounded: int32 [1024, 2048], P('gx', 'gy'), may hold values 0 or 1
Outputs:
- basis: float32 [32, 1024, 2048], P('dir', 'gx', 'gy')
- upper: float32 [32, 32], replicated
All inputs are finite; a program needn't handle non-finite values. No bound on the sum of `ice_mask` or of `grounded` on one device may be relied on, other than what follows from the above.
Results may differ from a plain program's by a relative error of at most 0.00021.
Values sent between devices are 32-bit elements; how exact they have to be, the bound alone decides.
A program may use at most 64 MiB of HBM per device.

v0:
```python
import jax
import jax.numpy as jnp
from jax import lax
from jax.sharding import PartitionSpec as P

SWEEPS = 6
damping = 0.8


def with_halo(value, sides, width):
    for axis, dim in sides:
        count, length = (lax.axis_size(axis), value.shape[dim])
        up = [(i, (i + 1) % count) for i in range(count - 1)]
        down = [(j, i) for i, j in up]
        last = lax.slice_in_dim(value, length - width, length, axis=dim)
        first = lax.slice_in_dim(value, 0, width, axis=dim)
        before = lax.ppermute(last, axis, up)
        after = lax.ppermute(first, axis, down)
        value = jnp.concatenate([before, value, after], axis=dim)
    return value


def weights_pair():
    along_x = jnp.array([4.0, 1.0], jnp.float32).reshape(2, 1, 1)
    along_y = jnp.array([1.0, 4.0], jnp.float32).reshape(2, 1, 1)
    return (along_x, along_y)


def relax_sweep(state, padded, coeffs, source):
    face_east, face_west, face_north, face_south, friction, diagonal, ice_keep = coeffs
    along_x, along_y = weights_pair()
    next_row = padded[..., 2:, 1:-1]
    prev_row = padded[..., :-2, 1:-1]
    next_col = padded[..., 1:-1, 2:]
    prev_col = padded[..., 1:-1, :-2]
    applied = along_x * (face_east * (state - next_row) + face_west * (state - prev_row))
    applied = applied + along_y * (
        face_north * (state - next_col) + face_south * (state - prev_col)
    )
    applied = applied + friction * state
    return ice_keep * (state + damping * (source - applied) / diagonal)


def solve_shared(source, coeffs):
    diagonal, ice_keep = (coeffs[5], coeffs[6])
    state = ice_keep * damping * source / diagonal
    for sweep in range(SWEEPS - 1):
        padded = with_halo(state, (("gx", 2), ("gy", 3)), 1)
        state = relax_sweep(state, padded, coeffs, source)
    return state


def make_coeffs(viscosity, padded_visc, basal_drag, grounded_f):
    face_east = 0.5 * (viscosity + padded_visc[2:, 1:-1])
    face_west = 0.5 * (viscosity + padded_visc[:-2, 1:-1])
    face_north = 0.5 * (viscosity + padded_visc[1:-1, 2:])
    face_south = 0.5 * (viscosity + padded_visc[1:-1, :-2])
    friction = basal_drag * grounded_f
    along_x, along_y = weights_pair()
    diagonal = along_x * (face_east + face_west) + along_y * (face_north + face_south) + friction
    return (face_east, face_west, face_north, face_south, friction, diagonal)


def on_device(directions, velocity, viscosity, basal_drag, misfit_weight, ice_mask, grounded):
    own_count = directions.shape[0]
    tile_rows = directions.shape[1]
    tile_cols = directions.shape[2]
    padded_visc = with_halo(viscosity, (("gx", 0), ("gy", 1)), 1)
    ice_keep = ice_mask.astype(jnp.float32)
    face_east, face_west, face_north, face_south, friction, diagonal = make_coeffs(
        viscosity, padded_visc, basal_drag, grounded.astype(jnp.float32)
    )
    coeffs = (face_east, face_west, face_north, face_south, friction, diagonal, ice_keep)
    forward = solve_shared(-friction * velocity[None] * directions[:, None], coeffs)
    adjoint = solve_shared(misfit_weight * forward, coeffs)
    sketch = -friction * jnp.sum(velocity[None] * adjoint, axis=1)
    cells = tile_rows * tile_cols
    total_cells = cells * lax.axis_size("gx") * lax.axis_size("gy")
    own_flat = sketch.reshape(own_count, cells)
    identity = jnp.eye(own_count * lax.axis_size("dir"), dtype=jnp.float32)
    whole = lax.all_gather(own_flat, "dir", axis=0, tiled=True)
    gram_local = jnp.dot(
        whole, whole.T, precision=lax.Precision.HIGHEST, preferred_element_type=jnp.float32
    )
    gram_sum = lax.psum(gram_local, ("gx", "gy"))
    lower = jnp.linalg.cholesky(gram_sum / jnp.float32(total_cells))
    inverse = lax.linalg.triangular_solve(lower, identity, left_side=True, lower=True)
    own_rows = lax.dynamic_slice_in_dim(inverse, lax.axis_index("dir") * own_count, own_count, 0)
    basis_flat = jnp.dot(
        own_rows, whole, precision=lax.Precision.HIGHEST, preferred_element_type=jnp.float32
    )
    return (basis_flat.reshape(own_count, tile_rows, tile_cols), lower.T)


def solution(mesh):
    placed = (
        P("dir", "gx", "gy"),
        P(None, "gx", "gy"),
        P("gx", "gy"),
        P("gx", "gy"),
        P("gx", "gy"),
        P("gx", "gy"),
        P("gx", "gy"),
    )
    return jax.shard_map(
        on_device,
        mesh=mesh,
        in_specs=placed,
        out_specs=(P("dir", "gx", "gy"), P()),
        check_vma=False,
    )
```

profile of v0, /device:TPU:64, one launch (start us, length us, event | category | flops | bytes accessed | tf_op | source)
XLA Modules:
  0.0 741.2 jit_solution(18365183644680429997)
XLA Ops:
  9.3 4.5 collective-permute-start.1
  25.3 4.5 collective-permute-start.5
  44.3 7.2 fusion.4
  52.8 5.0 collective-permute-start.9
  67.7 4.8 collective-permute-start.11
  77.2 5.3 fusion.8
  83.9 4.8 collective-permute-start.13
  98.7 4.1 collective-permute-start.15
  107.6 5.3 fusion.12
  114.2 6.7 collective-permute-start.17
  131.0 3.6 collective-permute-start.19
  139.4 5.3 fusion.16
  146.0 6.9 collective-permute-start.21
  166.7 8.1 %multiply_divide_fusion = (f32[8,2,128,256]{3,0,2,1:T(8,128)S(1)}, f32[8,2,128,256]{3,0,2,1:T(8,128)S(1)}) fusion(f32[2,128,256]{2,1,0:T(8,128)S(1)} %get-tuple-element.69, f32[128,256]{1,0:T(8,128)} %copy-done.17, f32[8,2,128,256]{3,0,2,1:T(8,128)} %copy-done.9, f32[128,256]{1,0:T(8,128)S(1)} %get-tuple-element.11, ...), kind=kLoop, calls=%fused_computation.279 | loop fusion | flops 16777216 | bytes 8962320 | tf_op jit(solution)/shard_map/div | solution.py:46
  176.1 6.7 collective-permute-start.25
  198.2 7.3 fusion.182
  206.9 6.9 collective-permute-start.29
  222.2 4.0 collective-permute-start.31
  229.5 7.0 fusion.183
  237.8 6.7 collective-permute-start.33
  252.8 3.8 collective-permute-start.35
  260.0 7.0 fusion.184
  268.3 6.9 collective-permute-start.37
  283.8 4.0 collective-permute-start.39
  291.2 7.0 fusion.185
  299.5 6.9 collective-permute-start.41
  316.4 4.6 collective-permute-start.43
  326.7 7.1 multiply_reduce_fusion
  335.0 99.5 %all-gather.2.cloned.1.call-done = f32[32,32768]{1,0:T(8,128)} async-done(((f32[8,32768]{1,0:T(8,128)}), f32[32,32768]{1,0:T(8,128)}) %all-gather.2.cloned.1.call-update) | async-done | bytes 4194320 | tf_op jit(solution)/shard_map/all_gather | solution.py:81
  434.4 6.9 fusion.230
  441.4 279.7 %psum.7 = f32[32,32]{0,1:T(8,128)S(1)} all-reduce(f32[32,32]{0,1:T(8,128)S(1)} %fusion.230), channel_id=1, replica_groups=mesh['gx'=8,'gy'=8,'dir'=4] {'gx','gy'}, use_global_device_ids=true, to_apply=%region_1.0 | all-reduce | flops 1024 | bytes 8192 | tf_op jit(solution)/shard_map/psum | solution.py:85
  728.1 3.8 fusion.198
  (232 shorter events, 173.5 us)
Async XLA Ops:
  7.2 427.3 %all-gather.2.cloned.1.call-start = ((), (), s32[]{:S(2)}) async-start(), calls=%async_computation | async-start | bytes 5242880 | tf_op jit(solution)/shard_map/all_gather | solution.py:81
  8.0 7.5 %collective-permute-start = (f32[1,256]{1,0:T(1,128)S(1)}, f32[1,256]{1,0:T(1,128)S(1)}, u32[]{:S(2)}, u32[]{:S(2)}) collective-permute-start(f32[1,256]{1,0:T(1,128)S(1)} %get-tuple-element.66), channel_id=1, source_target_pairs={{32,0},{64,32},{96,64},{128,96},{160,128},{192,160},{224,192},{33,... | collective-permute-start | bytes 3080 | tf_op jit(solution)/shard_map/ppermute | solution.py:18
  9.3 6.2 collective-permute-start.1
  51.5 6.3 collective-permute-start.8
  52.8 6.4 collective-permute-start.9
  64.0 8.6 %collective-permute-start.10 = (f32[8,2,130,1]{2,0,3,1:T(8,128)}, f32[8,2,130,1]{2,0,3,1:T(8,128)}, u32[]{:S(2)}, u32[]{:S(2)}) collective-permute-start(f32[8,2,130,1]{2,0,3,1:T(8,128)} %copy.104), channel_id=1, source_target_pairs={{4,0},{8,4},{12,8},{16,12},{20,16},{24,20},{28,24},{5,1},{9,5},{13... | collective-permute-start | bytes 24968 | tf_op jit(solution)/shard_map/ppermute | solution.py:18
  67.7 7.2 collective-permute-start.11
  82.6 6.1 collective-permute-start.12
  83.9 6.2 collective-permute-start.13
  95.0 7.9 %collective-permute-start.14 = (f32[8,2,130,1]{2,0,3,1:T(8,128)}, f32[8,2,130,1]{2,0,3,1:T(8,128)}, u32[]{:S(2)}, u32[]{:S(2)}) collective-permute-start(f32[8,2,130,1]{2,0,3,1:T(8,128)} %copy.108), channel_id=1, source_target_pairs={{4,0},{8,4},{12,8},{16,12},{20,16},{24,20},{28,24},{5,1},{9,5},{13... | collective-permute-start | bytes 24968 | tf_op jit(solution)/shard_map/ppermute | solution.py:18
  98.7 6.5 collective-permute-start.15
  112.9 8.0 %collective-permute-start.16 = (f32[8,2,1,256]{3,0,2,1:T(8,128)S(1)}, f32[8,2,1,256]{3,0,2,1:T(8,128)S(1)}, u32[]{:S(2)}, u32[]{:S(2)}) collective-permute-start(f32[8,2,1,256]{3,0,2,1:T(8,128)S(1)} %get-tuple-element.53), channel_id=1, source_target_pairs={{32,0},{64,32},{96,64},{128,96},{160,128},{192,160},{224,192},{33,... | collective-permute-start | bytes 49160 | tf_op jit(solution)/shard_map/ppermute | solution.py:18
  114.2 8.1 %collective-permute-start.17 = (f32[8,2,1,256]{3,0,2,1:T(8,128)S(1)}, f32[8,2,1,256]{3,0,2,1:T(8,128)S(1)}, u32[]{:S(2)}, u32[]{:S(2)}) collective-permute-start(f32[8,2,1,256]{3,0,2,1:T(8,128)S(1)} %get-tuple-element.52), channel_id=1, source_target_pairs={{0,32},{32,64},{64,96},{96,128},{128,160},{160,192},{192,224},{1,3... | collective-permute-start | bytes 49160 | tf_op jit(solution)/shard_map/ppermute | solution.py:17
  127.2 7.4 collective-permute-start.18
  144.7 8.2 %collective-permute-start.20 = (f32[8,2,1,256]{3,0,2,1:T(8,128)S(1)}, f32[8,2,1,256]{3,0,2,1:T(8,128)S(1)}, u32[]{:S(2)}, u32[]{:S(2)}) collective-permute-start(f32[8,2,1,256]{3,0,2,1:T(8,128)S(1)} %get-tuple-element.51), channel_id=1, source_target_pairs={{32,0},{64,32},{96,64},{128,96},{160,128},{192,160},{224,192},{33,... | collective-permute-start | bytes 49160 | tf_op jit(solution)/shard_map/ppermute | solution.py:18
  146.0 8.4 %collective-permute-start.21 = (f32[8,2,1,256]{3,0,2,1:T(8,128)S(1)}, f32[8,2,1,256]{3,0,2,1:T(8,128)S(1)}, u32[]{:S(2)}, u32[]{:S(2)}) collective-permute-start(f32[8,2,1,256]{3,0,2,1:T(8,128)S(1)} %get-tuple-element.50), channel_id=1, source_target_pairs={{0,32},{32,64},{64,96},{96,128},{128,160},{160,192},{192,224},{1,3... | collective-permute-start | bytes 49160 | tf_op jit(solution)/shard_map/ppermute | solution.py:17
  174.8 8.0 %collective-permute-start.24 = (f32[8,2,1,256]{3,0,2,1:T(8,128)S(1)}, f32[8,2,1,256]{3,0,2,1:T(8,128)S(1)}, u32[]{:S(2)}, u32[]{:S(2)}) collective-permute-start(f32[8,2,1,256]{3,0,2,1:T(8,128)S(1)} %get-tuple-element.49), channel_id=1, source_target_pairs={{32,0},{64,32},{96,64},{128,96},{160,128},{192,160},{224,192},{33,... | collective-permute-start | bytes 49160 | tf_op jit(solution)/shard_map/ppermute | solution.py:18
  176.1 8.1 %collective-permute-start.25 = (f32[8,2,1,256]{3,0,2,1:T(8,128)S(1)}, f32[8,2,1,256]{3,0,2,1:T(8,128)S(1)}, u32[]{:S(2)}, u32[]{:S(2)}) collective-permute-start(f32[8,2,1,256]{3,0,2,1:T(8,128)S(1)} %get-tuple-element.48), channel_id=1, source_target_pairs={{0,32},{32,64},{64,96},{96,128},{128,160},{160,192},{192,224},{1,3... | collective-permute-start | bytes 49160 | tf_op jit(solution)/shard_map/ppermute | solution.py:17
  188.1 6.8 collective-permute-start.26
  205.6 8.2 %collective-permute-start.28 = (f32[8,2,1,256]{3,0,2,1:T(8,128)S(1)}, f32[8,2,1,256]{3,0,2,1:T(8,128)S(1)}, u32[]{:S(2)}, u32[]{:S(2)}) collective-permute-start(f32[8,2,1,256]{3,0,2,1:T(8,128)S(1)} %get-tuple-element.47), channel_id=1, source_target_pairs={{32,0},{64,32},{96,64},{128,96},{160,128},{192,160},{224,192},{33,... | collective-permute-start | bytes 49160 | tf_op jit(solution)/shard_map/ppermute | solution.py:18
  206.9 8.4 %collective-permute-start.29 = (f32[8,2,1,256]{3,0,2,1:T(8,128)S(1)}, f32[8,2,1,256]{3,0,2,1:T(8,128)S(1)}, u32[]{:S(2)}, u32[]{:S(2)}) collective-permute-start(f32[8,2,1,256]{3,0,2,1:T(8,128)S(1)} %get-tuple-element.46), channel_id=1, source_target_pairs={{0,32},{32,64},{64,96},{96,128},{128,160},{160,192},{192,224},{1,3... | collective-permute-start | bytes 49160 | tf_op jit(solution)/shard_map/ppermute | solution.py:17
  219.0 7.2 collective-permute-start.30
  236.6 8.0 %collective-permute-start.32 = (f32[8,2,1,256]{3,0,2,1:T(8,128)S(1)}, f32[8,2,1,256]{3,0,2,1:T(8,128)S(1)}, u32[]{:S(2)}, u32[]{:S(2)}) collective-permute-start(f32[8,2,1,256]{3,0,2,1:T(8,128)S(1)} %get-tuple-element.45), channel_id=1, source_target_pairs={{32,0},{64,32},{96,64},{128,96},{160,128},{192,160},{224,192},{33,... | collective-permute-start | bytes 49160 | tf_op jit(solution)/shard_map/ppermute | solution.py:18
  237.8 8.1 %collective-permute-start.33 = (f32[8,2,1,256]{3,0,2,1:T(8,128)S(1)}, f32[8,2,1,256]{3,0,2,1:T(8,128)S(1)}, u32[]{:S(2)}, u32[]{:S(2)}) collective-permute-start(f32[8,2,1,256]{3,0,2,1:T(8,128)S(1)} %get-tuple-element.44), channel_id=1, source_target_pairs={{0,32},{32,64},{64,96},{96,128},{128,160},{160,192},{192,224},{1,3... | collective-permute-start | bytes 49160 | tf_op jit(solution)/shard_map/ppermute | solution.py:17
  249.7 7.0 collective-permute-start.34
  267.0 8.2 %collective-permute-start.36 = (f32[8,2,1,256]{3,0,2,1:T(8,128)S(1)}, f32[8,2,1,256]{3,0,2,1:T(8,128)S(1)}, u32[]{:S(2)}, u32[]{:S(2)}) collective-permute-start(f32[8,2,1,256]{3,0,2,1:T(8,128)S(1)} %get-tuple-element.43), channel_id=1, source_target_pairs={{32,0},{64,32},{96,64},{128,96},{160,128},{192,160},{224,192},{33,... | collective-permute-start | bytes 49160 | tf_op jit(solution)/shard_map/ppermute | solution.py:18
  268.3 8.4 %collective-permute-start.37 = (f32[8,2,1,256]{3,0,2,1:T(8,128)S(1)}, f32[8,2,1,256]{3,0,2,1:T(8,128)S(1)}, u32[]{:S(2)}, u32[]{:S(2)}) collective-permute-start(f32[8,2,1,256]{3,0,2,1:T(8,128)S(1)} %get-tuple-element.42), channel_id=1, source_target_pairs={{0,32},{32,64},{64,96},{96,128},{128,160},{160,192},{192,224},{1,3... | collective-permute-start | bytes 49160 | tf_op jit(solution)/shard_map/ppermute | solution.py:17
  280.4 7.4 collective-permute-start.38
  298.2 8.2 %collective-permute-start.40 = (f32[8,2,1,256]{3,0,2,1:T(8,128)S(1)}, f32[8,2,1,256]{3,0,2,1:T(8,128)S(1)}, u32[]{:S(2)}, u32[]{:S(2)}) collective-permute-start(f32[8,2,1,256]{3,0,2,1:T(8,128)S(1)} %get-tuple-element.41), channel_id=1, source_target_pairs={{32,0},{64,32},{96,64},{128,96},{160,128},{192,160},{224,192},{33,... | collective-permute-start | bytes 49160 | tf_op jit(solution)/shard_map/ppermute | solution.py:18
  299.5 8.4 %collective-permute-start.41 = (f32[8,2,1,256]{3,0,2,1:T(8,128)S(1)}, f32[8,2,1,256]{3,0,2,1:T(8,128)S(1)}, u32[]{:S(2)}, u32[]{:S(2)}) collective-permute-start(f32[8,2,1,256]{3,0,2,1:T(8,128)S(1)} %get-tuple-element.40), channel_id=1, source_target_pairs={{0,32},{32,64},{64,96},{96,128},{128,160},{160,192},{192,224},{1,3... | collective-permute-start | bytes 49160 | tf_op jit(solution)/shard_map/ppermute | solution.py:17
  312.6 9.3 %collective-permute-start.42 = (f32[8,2,130,1]{2,0,3,1:T(8,128)}, f32[8,2,130,1]{2,0,3,1:T(8,128)}, u32[]{:S(2)}, u32[]{:S(2)}) collective-permute-start(f32[8,2,130,1]{2,0,3,1:T(8,128)} %copy.136), channel_id=1, source_target_pairs={{4,0},{8,4},{12,8},{16,12},{20,16},{24,20},{28,24},{5,1},{9,5},{13... | collective-permute-start | bytes 24968 | tf_op jit(solution)/shard_map/ppermute | solution.py:18
  316.4 7.9 %collective-permute-start.43 = (f32[8,2,130,1]{2,0,3,1:T(8,128)}, f32[8,2,130,1]{2,0,3,1:T(8,128)}, u32[]{:S(2)}, u32[]{:S(2)}) collective-permute-start(f32[8,2,130,1]{2,0,3,1:T(8,128)} %copy.138), channel_id=1, source_target_pairs={{0,4},{4,8},{8,12},{12,16},{16,20},{20,24},{24,28},{1,5},{5,9},{9,... | collective-permute-start | bytes 24968 | tf_op jit(solution)/shard_map/ppermute | solution.py:17
  (46 other events, 361.7 us)
Sparse Core Ops, SparseCore 0:
  335.1 99.3 all-gather.1
where the time goes:
time: 752 us; the launch traced here: 741 us
  blocking collectives  280 us (37%)
  starting transfers between devices  137 us (18%)
  waiting for transfers between devices  114 us (15%)
  local copies, waits for them, and re-layouts  103 us (14%)
  other arithmetic  81.4 us (11%)
  between operations  15.5 us (2%)
  matrix products  11 us (1%)
    psum x1, blocking collectives, on_device(): gram_sum = lax.psum(gram_local, ('gx', 'gy'))  280 us
    ppermute x22, starting transfers between devices, with_halo(): before = lax.ppermute(last, axis, up)  108 us
    all_gather x1, waiting for transfers between devices, on_device(): whole = lax.all_gather(own_flat, 'dir', axis=0, tiled=True)  99.5 us
    mul x8, other arithmetic, relax_sweep(): return ice_keep * (state + damping * (source - applied) / diagonal)  51.3 us
    slice x21, local copies, waits for them, and re-layouts, with_halo(): first = lax.slice_in_dim(value, 0, width, axis=dim)  37.7 us
    ppermute x22, starting transfers between devices, with_halo(): after = lax.ppermute(first, axis, down)  28.6 us
    slice x21, local copies, waits for them, and re-layouts, with_halo(): last = lax.slice_in_dim(value, length - width, length, axis=dim)  19.6 us
    ppermute x10, local copies, waits for them, and re-layouts, with_halo(): after = lax.ppermute(first, axis, down)  19.5 us
  transfers between devices with their start and end apart: 45, of which 11 were waited for; matrix products, arithmetic and copies ran while one was open for 6% of the time, Pallas kernels for 0%

commit v1 on v0

--- a/solution.py
+++ b/solution.py
@@ -82,7 +82,8 @@
     gram_local = jnp.dot(
         whole, whole.T, precision=lax.Precision.HIGHEST, preferred_element_type=jnp.float32
     )
-    gram_sum = lax.psum(gram_local, ("gx", "gy"))
+    extra = lax.all_gather(gram_local, ("gx", "gy"))
+    gram_sum = jnp.sum(extra, 0)
     lower = jnp.linalg.cholesky(gram_sum / jnp.float32(total_cells))
     inverse = lax.linalg.triangular_solve(lower, identity, left_side=True, lower=True)
     own_rows = lax.dynamic_slice_in_dim(inverse, lax.axis_index("dir") * own_count, own_count, 0)

time: 752 us -> 560 us (0.74)
  the two profiles are of different devices: /device:TPU:64 before, /device:TPU:1 now
where the time goes in v1:
time: 560 us; the launch traced here: 549 us
  starting transfers between devices  145 us (26%)
  local copies, waits for them, and re-layouts  103 us (18%)
  waiting for transfers between devices  99 us (18%)
  blocking collectives  93.9 us (17%)
  other arithmetic  81.5 us (15%)
  between operations  15.6 us (3%)
  matrix products  11 us (2%)
    ppermute x22, starting transfers between devices, with_halo(): before = lax.ppermute(last, axis, up)  106 us
    all_gather x1, blocking collectives, on_device(): extra = lax.all_gather(gram_local, ('gx', 'gy'))  93.9 us
    all_gather x1, waiting for transfers between devices, on_device(): whole = lax.all_gather(own_flat, 'dir', axis=0, tiled=True)  89.7 us
    mul x8, other arithmetic, relax_sweep(): return ice_keep * (state + damping * (source - applied) / diagonal)  51.3 us
    ppermute x22, starting transfers between devices, with_halo(): after = lax.ppermute(first, axis, down)  39 us
    slice x21, local copies, waits for them, and re-layouts, with_halo(): first = lax.slice_in_dim(value, 0, width, axis=dim)  36.5 us
    slice x21, local copies, waits for them, and re-layouts, with_halo(): last = lax.slice_in_dim(value, length - width, length, axis=dim)  20.8 us
    ppermute x10, local copies, waits for them, and re-layouts, with_halo(): after = lax.ppermute(first, axis, down)  19.5 us
  transfers between devices with their start and end apart: 45, of which 12 were waited for; matrix products, arithmetic and copies ran while one was open for 8% of the time, Pallas kernels for 0%

profile of v1, /device:TPU:1, one launch (start us, length us, event | category | flops | bytes accessed | tf_op | source)
XLA Modules:
  0.0 549.3 jit_solution(16831875382917702248)
XLA Ops:
  9.3 4.7 collective-permute-start.1
  16.7 5.0 collective-permute-start.2
  28.0 4.1 collective-permute-start.5
  37.0 5.0 collective-permute-start.7
  49.4 7.2 %fusion.4 = f32[8,2,128,256]{3,0,2,1:T(8,128)S(1)} fusion(f32[8,2,128,256]{3,0,2,1:T(8,128)} %copy-done.8, f32[8,2,130,1]{3,0,2,1:T(8,128)} %copy.100, f32[8,2,1,256]{3,0,2,1:T(8,128)S(1)} %collective-permute-done.4, f32[8,2,1,256]{3,0,2,1:T(8,128)} %copy-done.25, f32[8,2,130,1]{3,0,2,1:T(8,128)} %copy.98, f32[128,256]{1,0:T(8,128)S(1)} %get-tuple-element.11, ...), kind=kLoop, calls=%fused_computation.20 | loop fusion | flops 15204352 | bytes 6603024 | tf_op jit(solution)/shard_map/mul | solution.py:41
  58.0 4.5 collective-permute-start.9
  80.9 5.3 fusion.8
  87.5 4.5 collective-permute-start.13
  102.2 4.4 collective-permute-start.15
  111.4 5.3 fusion.12
  118.0 5.7 %collective-permute-start.17 = (f32[8,2,1,256]{3,0,2,1:T(8,128)S(1)}, f32[8,2,1,256]{3,0,2,1:T(8,128)S(1)}, u32[]{:S(2)}, u32[]{:S(2)}) collective-permute-start(f32[8,2,1,256]{3,0,2,1:T(8,128)S(1)} %get-tuple-element.52), channel_id=1, source_target_pairs={{0,32},{32,64},{64,96},{96,128},{128,160},{160,192},{192,224},{1,3... | collective-permute-start | bytes 49160 | tf_op jit(solution)/shard_map/ppermute | solution.py:17
  142.2 5.3 fusion.16
  148.8 6.7 %collective-permute-start.21 = (f32[8,2,1,256]{3,0,2,1:T(8,128)S(1)}, f32[8,2,1,256]{3,0,2,1:T(8,128)S(1)}, u32[]{:S(2)}, u32[]{:S(2)}) collective-permute-start(f32[8,2,1,256]{3,0,2,1:T(8,128)S(1)} %get-tuple-element.50), channel_id=1, source_target_pairs={{0,32},{32,64},{64,96},{96,128},{128,160},{160,192},{192,224},{1,3... | collective-permute-start | bytes 49160 | tf_op jit(solution)/shard_map/ppermute | solution.py:17
  170.1 8.1 %multiply_divide_fusion = (f32[8,2,128,256]{3,0,2,1:T(8,128)S(1)}, f32[8,2,128,256]{3,0,2,1:T(8,128)S(1)}) fusion(f32[2,128,256]{2,1,0:T(8,128)S(1)} %get-tuple-element.69, f32[128,256]{1,0:T(8,128)} %copy-done.17, f32[8,2,128,256]{3,0,2,1:T(8,128)} %copy-done.9, f32[128,256]{1,0:T(8,128)S(1)} %get-tuple-element.11, ...), kind=kLoop, calls=%fused_computation.279 | loop fusion | flops 16777216 | bytes 8962320 | tf_op jit(solution)/shard_map/div | solution.py:46
  179.5 6.7 %collective-permute-start.25 = (f32[8,2,1,256]{3,0,2,1:T(8,128)S(1)}, f32[8,2,1,256]{3,0,2,1:T(8,128)S(1)}, u32[]{:S(2)}, u32[]{:S(2)}) collective-permute-start(f32[8,2,1,256]{3,0,2,1:T(8,128)S(1)} %get-tuple-element.48), channel_id=1, source_target_pairs={{0,32},{32,64},{64,96},{96,128},{128,160},{160,192},{192,224},{1,3... | collective-permute-start | bytes 49160 | tf_op jit(solution)/shard_map/ppermute | solution.py:17
  194.7 4.4 collective-permute-start.27
  202.5 7.3 %fusion.182 = f32[8,2,128,256]{3,0,2,1:T(8,128)S(1)} fusion(f32[8,2,128,256]{3,0,2,1:T(8,128)} %copy-done.10, f32[8,2,128,256]{3,0,2,1:T(8,128)S(1)} %get-tuple-element.13, f32[8,2,1,256]{3,0,2,1:T(8,128)S(1)} %collective-permute-done.24, f32[8,2,1,256]{3,0,2,1:T(8,128)S(1)} %collective-permute-done.25, f32[8,2,130,1]{3,0,2,1:T(8,128)} %copy.120, ...), kind=kLoop, calls=%fused_computation.280 | loop fusion | flops 14680064 | bytes 7389456 | tf_op jit(solution)/shard_map/mul | solution.py:41
  211.2 6.7 %collective-permute-start.29 = (f32[8,2,1,256]{3,0,2,1:T(8,128)S(1)}, f32[8,2,1,256]{3,0,2,1:T(8,128)S(1)}, u32[]{:S(2)}, u32[]{:S(2)}) collective-permute-start(f32[8,2,1,256]{3,0,2,1:T(8,128)S(1)} %get-tuple-element.46), channel_id=1, source_target_pairs={{0,32},{32,64},{64,96},{96,128},{128,160},{160,192},{192,224},{1,3... | collective-permute-start | bytes 49160 | tf_op jit(solution)/shard_map/ppermute | solution.py:17
  226.2 4.0 collective-permute-start.31
  233.6 7.0 %fusion.183 = f32[8,2,128,256]{3,0,2,1:T(8,128)S(1)} fusion(f32[8,2,128,256]{3,0,2,1:T(8,128)} %copy-done.5, f32[8,2,128,256]{3,0,2,1:T(8,128)S(1)} %get-tuple-element.13, f32[8,2,1,256]{3,0,2,1:T(8,128)S(1)} %collective-permute-done.28, f32[8,2,1,256]{3,0,2,1:T(8,128)S(1)} %collective-permute-done.29, f32[8,2,130,1]{3,0,2,1:T(8,128)} %copy.124, ...), kind=kLoop, calls=%fused_computation.281 | loop fusion | flops 14680064 | bytes 7389456 | tf_op jit(solution)/shard_map/mul | solution.py:41
  241.9 6.4 %collective-permute-start.33 = (f32[8,2,1,256]{3,0,2,1:T(8,128)S(1)}, f32[8,2,1,256]{3,0,2,1:T(8,128)S(1)}, u32[]{:S(2)}, u32[]{:S(2)}) collective-permute-start(f32[8,2,1,256]{3,0,2,1:T(8,128)S(1)} %get-tuple-element.44), channel_id=1, source_target_pairs={{0,32},{32,64},{64,96},{96,128},{128,160},{160,192},{192,224},{1,3... | collective-permute-start | bytes 49160 | tf_op jit(solution)/shard_map/ppermute | solution.py:17
  256.7 4.2 collective-permute-start.35
  264.3 7.0 %fusion.184 = f32[8,2,128,256]{3,0,2,1:T(8,128)S(1)} fusion(f32[8,2,128,256]{3,0,2,1:T(8,128)} %copy-done.6, f32[8,2,128,256]{3,0,2,1:T(8,128)S(1)} %get-tuple-element.13, f32[8,2,1,256]{3,0,2,1:T(8,128)S(1)} %collective-permute-done.32, f32[8,2,1,256]{3,0,2,1:T(8,128)S(1)} %collective-permute-done.33, f32[8,2,130,1]{3,0,2,1:T(8,128)} %copy.128, ...), kind=kLoop, calls=%fused_computation.282 | loop fusion | flops 14680064 | bytes 7389456 | tf_op jit(solution)/shard_map/mul | solution.py:41
  272.6 6.7 %collective-permute-start.37 = (f32[8,2,1,256]{3,0,2,1:T(8,128)S(1)}, f32[8,2,1,256]{3,0,2,1:T(8,128)S(1)}, u32[]{:S(2)}, u32[]{:S(2)}) collective-permute-start(f32[8,2,1,256]{3,0,2,1:T(8,128)S(1)} %get-tuple-element.42), channel_id=1, source_target_pairs={{0,32},{32,64},{64,96},{96,128},{128,160},{160,192},{192,224},{1,3... | collective-permute-start | bytes 49160 | tf_op jit(solution)/shard_map/ppermute | solution.py:17
  287.8 4.2 collective-permute-start.39
  295.4 7.0 %fusion.185 = f32[8,2,128,256]{3,0,2,1:T(8,128)S(1)} fusion(f32[8,2,128,256]{3,0,2,1:T(8,128)} %copy-done.7, f32[8,2,128,256]{3,0,2,1:T(8,128)S(1)} %get-tuple-element.13, f32[8,2,1,256]{3,0,2,1:T(8,128)S(1)} %collective-permute-done.36, f32[8,2,1,256]{3,0,2,1:T(8,128)S(1)} %collective-permute-done.37, f32[8,2,130,1]{3,0,2,1:T(8,128)} %copy.132, ...), kind=kLoop, calls=%fused_computation.283 | loop fusion | flops 14680064 | bytes 7389456 | tf_op jit(solution)/shard_map/mul | solution.py:41
  303.7 6.7 %collective-permute-start.41 = (f32[8,2,1,256]{3,0,2,1:T(8,128)S(1)}, f32[8,2,1,256]{3,0,2,1:T(8,128)S(1)}, u32[]{:S(2)}, u32[]{:S(2)}) collective-permute-start(f32[8,2,1,256]{3,0,2,1:T(8,128)S(1)} %get-tuple-element.40), channel_id=1, source_target_pairs={{0,32},{32,64},{64,96},{96,128},{128,160},{160,192},{192,224},{1,3... | collective-permute-start | bytes 49160 | tf_op jit(solution)/shard_map/ppermute | solution.py:17
  320.4 4.2 collective-permute-start.43
  330.3 7.1 %multiply_reduce_fusion = f32[8,128,256]{2,0,1:T(8,128)S(1)} fusion(f32[8,2,128,256]{3,0,2,1:T(8,128)} %copy-done, f32[8,2,128,256]{3,0,2,1:T(8,128)S(1)} %get-tuple-element.13, f32[8,2,1,256]{3,0,2,1:T(8,128)S(1)} %collective-permute-done.40, f32[8,2,1,256]{3,0,2,1:T(8,128)} %copy-done.23, f32[8,2,130,1]{3,0,2,1:T(8,128)} %copy.136, ...), kind=kLoop, calls=%fused_computation.278 | loop fusion | flops 15466496 | bytes 6603024 | tf_op jit(solution)/shard_map/reduce_sum | solution.py:76
  338.6 89.7 %all-gather.3.cloned.1.call-done = f32[32,32768]{1,0:T(8,128)} async-done(((f32[8,32768]{1,0:T(8,128)}), f32[32,32768]{1,0:T(8,128)}) %all-gather.3.cloned.1.call-update) | async-done | bytes 4194320 | tf_op jit(solution)/shard_map/all_gather | solution.py:81
  428.3 6.9 %fusion.230 = f32[32,32]{1,0:T(8,128)S(1)} fusion(f32[32,32768]{1,0:T(8,128)} %all-gather.3.cloned.1.call-done), kind=kOutput, calls=%fused_computation.345 | convolution fusion | flops 402653184 | bytes 4198400 | tf_op jit(solution)/shard_map/dot_general | solution.py:82
  435.3 93.9 %all-gather = f32[2048,32]{1,0:T(8,128)S(1)} all-gather(f32[32,32]{1,0:T(8,128)S(1)} %fusion.230), channel_id=2, replica_groups=mesh['gx'=8,'gy'=8,'dir'=4] {'gx','gy'}, dimensions={0}, use_global_device_ids=true | all-gather | bytes 266240 | tf_op jit(solution)/shard_map/all_gather | solution.py:85
  (232 shorter events, 177.9 us)
Async XLA Ops:
  7.2 421.1 %all-gather.3.cloned.1.call-start = ((), (), s32[]{:S(2)}) async-start(), calls=%async_computation | async-start | bytes 5242880 | tf_op jit(solution)/shard_map/all_gather | solution.py:81
  8.0 7.6 %collective-permute-start = (f32[1,256]{1,0:T(1,128)S(1)}, f32[1,256]{1,0:T(1,128)S(1)}, u32[]{:S(2)}, u32[]{:S(2)}) collective-permute-start(f32[1,256]{1,0:T(1,128)S(1)} %get-tuple-element.66), channel_id=1, source_target_pairs={{32,0},{64,32},{96,64},{128,96},{160,128},{192,160},{224,192},{33,... | collective-permute-start | bytes 3080 | tf_op jit(solution)/shard_map/ppermute | solution.py:18
  9.3 6.3 %collective-permute-start.1 = (f32[1,256]{1,0:T(1,128)S(1)}, f32[1,256]{1,0:T(1,128)S(1)}, u32[]{:S(2)}, u32[]{:S(2)}) collective-permute-start(f32[1,256]{1,0:T(1,128)S(1)} %get-tuple-element.65), channel_id=1, source_target_pairs={{0,32},{32,64},{64,96},{96,128},{128,160},{160,192},{192,224},{1,3... | collective-permute-start | bytes 3080 | tf_op jit(solution)/shard_map/ppermute | solution.py:17
  16.7 8.6 %collective-permute-start.2 = (f32[130,1]{1,0:T(8,128)S(1)}, f32[130,1]{1,0:T(8,128)S(1)}, u32[]{:S(2)}, u32[]{:S(2)}) collective-permute-start(f32[130,1]{1,0:T(8,128)S(1)} %get-tuple-element.60), channel_id=1, source_target_pairs={{4,0},{8,4},{12,8},{16,12},{20,16},{24,20},{28,24},{5,1},{9,5},{13... | collective-permute-start | bytes 1568 | tf_op jit(solution)/shard_map/ppermute | solution.py:18
  37.0 8.3 %collective-permute-start.7 = (f32[8,2,130,1]{2,0,3,1:T(8,128)S(1)}, f32[8,2,130,1]{2,0,3,1:T(8,128)S(1)}, u32[]{:S(2)}, u32[]{:S(2)}) collective-permute-start(f32[8,2,130,1]{2,0,3,1:T(8,128)S(1)} %copy.99), channel_id=1, source_target_pairs={{0,4},{4,8},{8,12},{12,16},{16,20},{20,24},{24,28},{1,5},{5,9},{9,... | collective-permute-start | bytes 24968 | tf_op jit(solution)/shard_map/ppermute | solution.py:17
  68.1 8.1 %collective-permute-start.10 = (f32[8,2,130,1]{2,0,3,1:T(8,128)}, f32[8,2,130,1]{2,0,3,1:T(8,128)}, u32[]{:S(2)}, u32[]{:S(2)}) collective-permute-start(f32[8,2,130,1]{2,0,3,1:T(8,128)} %copy.101), channel_id=1, source_target_pairs={{4,0},{8,4},{12,8},{16,12},{20,16},{24,20},{28,24},{5,1},{9,5},{13... | collective-permute-start | bytes 24968 | tf_op jit(solution)/shard_map/ppermute | solution.py:18
  72.5 6.1 %collective-permute-start.11 = (f32[8,2,130,1]{2,0,3,1:T(8,128)}, f32[8,2,130,1]{2,0,3,1:T(8,128)}, u32[]{:S(2)}, u32[]{:S(2)}) collective-permute-start(f32[8,2,130,1]{2,0,3,1:T(8,128)} %copy.103), channel_id=1, source_target_pairs={{0,4},{4,8},{8,12},{12,16},{16,20},{20,24},{24,28},{1,5},{5,9},{9,... | collective-permute-start | bytes 24968 | tf_op jit(solution)/shard_map/ppermute | solution.py:17
  97.8 8.8 %collective-permute-start.14 = (f32[8,2,130,1]{2,0,3,1:T(8,128)}, f32[8,2,130,1]{2,0,3,1:T(8,128)}, u32[]{:S(2)}, u32[]{:S(2)}) collective-permute-start(f32[8,2,130,1]{2,0,3,1:T(8,128)} %copy.105), channel_id=1, source_target_pairs={{4,0},{8,4},{12,8},{16,12},{20,16},{24,20},{28,24},{5,1},{9,5},{13... | collective-permute-start | bytes 24968 | tf_op jit(solution)/shard_map/ppermute | solution.py:18
  102.2 6.8 %collective-permute-start.15 = (f32[8,2,130,1]{2,0,3,1:T(8,128)}, f32[8,2,130,1]{2,0,3,1:T(8,128)}, u32[]{:S(2)}, u32[]{:S(2)}) collective-permute-start(f32[8,2,130,1]{2,0,3,1:T(8,128)} %copy.107), channel_id=1, source_target_pairs={{0,4},{4,8},{8,12},{12,16},{16,20},{20,24},{24,28},{1,5},{5,9},{9,... | collective-permute-start | bytes 24968 | tf_op jit(solution)/shard_map/ppermute | solution.py:17
  116.7 7.0 %collective-permute-start.16 = (f32[8,2,1,256]{3,0,2,1:T(8,128)S(1)}, f32[8,2,1,256]{3,0,2,1:T(8,128)S(1)}, u32[]{:S(2)}, u32[]{:S(2)}) collective-permute-start(f32[8,2,1,256]{3,0,2,1:T(8,128)S(1)} %get-tuple-element.53), channel_id=1, source_target_pairs={{32,0},{64,32},{96,64},{128,96},{160,128},{192,160},{224,192},{33,... | collective-permute-start | bytes 49160 | tf_op jit(solution)/shard_map/ppermute | solution.py:18
  118.0 6.5 %collective-permute-start.17 = (f32[8,2,1,256]{3,0,2,1:T(8,128)S(1)}, f32[8,2,1,256]{3,0,2,1:T(8,128)S(1)}, u32[]{:S(2)}, u32[]{:S(2)}) collective-permute-start(f32[8,2,1,256]{3,0,2,1:T(8,128)S(1)} %get-tuple-element.52), channel_id=1, source_target_pairs={{0,32},{32,64},{64,96},{96,128},{128,160},{160,192},{192,224},{1,3... | collective-permute-start | bytes 49160 | tf_op jit(solution)/shard_map/ppermute | solution.py:17
  129.4 8.0 %collective-permute-start.18 = (f32[8,2,130,1]{2,0,3,1:T(8,128)}, f32[8,2,130,1]{2,0,3,1:T(8,128)}, u32[]{:S(2)}, u32[]{:S(2)}) collective-permute-start(f32[8,2,130,1]{2,0,3,1:T(8,128)} %copy.109), channel_id=1, source_target_pairs={{4,0},{8,4},{12,8},{16,12},{20,16},{24,20},{28,24},{5,1},{9,5},{13... | collective-permute-start | bytes 24968 | tf_op jit(solution)/shard_map/ppermute | solution.py:18
  147.5 8.0 %collective-permute-start.20 = (f32[8,2,1,256]{3,0,2,1:T(8,128)S(1)}, f32[8,2,1,256]{3,0,2,1:T(8,128)S(1)}, u32[]{:S(2)}, u32[]{:S(2)}) collective-permute-start(f32[8,2,1,256]{3,0,2,1:T(8,128)S(1)} %get-tuple-element.51), channel_id=1, source_target_pairs={{32,0},{64,32},{96,64},{128,96},{160,128},{192,160},{224,192},{33,... | collective-permute-start | bytes 49160 | tf_op jit(solution)/shard_map/ppermute | solution.py:18
  148.8 7.5 %collective-permute-start.21 = (f32[8,2,1,256]{3,0,2,1:T(8,128)S(1)}, f32[8,2,1,256]{3,0,2,1:T(8,128)S(1)}, u32[]{:S(2)}, u32[]{:S(2)}) collective-permute-start(f32[8,2,1,256]{3,0,2,1:T(8,128)S(1)} %get-tuple-element.50), channel_id=1, source_target_pairs={{0,32},{32,64},{64,96},{96,128},{128,160},{160,192},{192,224},{1,3... | collective-permute-start | bytes 49160 | tf_op jit(solution)/shard_map/ppermute | solution.py:17
  160.3 6.4 %collective-permute-start.22 = (f32[8,2,130,1]{2,0,3,1:T(8,128)S(1)}, f32[8,2,130,1]{2,0,3,1:T(8,128)S(1)}, u32[]{:S(2)}, u32[]{:S(2)}) collective-permute-start(f32[8,2,130,1]{2,0,3,1:T(8,128)S(1)} %copy.113), channel_id=1, source_target_pairs={{4,0},{8,4},{12,8},{16,12},{20,16},{24,20},{28,24},{5,1},{9,5},{13... | collective-permute-start | bytes 24968 | tf_op jit(solution)/shard_map/ppermute | solution.py:18
  178.2 8.0 %collective-permute-start.24 = (f32[8,2,1,256]{3,0,2,1:T(8,128)S(1)}, f32[8,2,1,256]{3,0,2,1:T(8,128)S(1)}, u32[]{:S(2)}, u32[]{:S(2)}) collective-permute-start(f32[8,2,1,256]{3,0,2,1:T(8,128)S(1)} %get-tuple-element.49), channel_id=1, source_target_pairs={{32,0},{64,32},{96,64},{128,96},{160,128},{192,160},{224,192},{33,... | collective-permute-start | bytes 49160 | tf_op jit(solution)/shard_map/ppermute | solution.py:18
  179.5 7.5 %collective-permute-start.25 = (f32[8,2,1,256]{3,0,2,1:T(8,128)S(1)}, f32[8,2,1,256]{3,0,2,1:T(8,128)S(1)}, u32[]{:S(2)}, u32[]{:S(2)}) collective-permute-start(f32[8,2,1,256]{3,0,2,1:T(8,128)S(1)} %get-tuple-element.48), channel_id=1, source_target_pairs={{0,32},{32,64},{64,96},{96,128},{128,160},{160,192},{192,224},{1,3... | collective-permute-start | bytes 49160 | tf_op jit(solution)/shard_map/ppermute | solution.py:17
  190.9 8.2 %collective-permute-start.26 = (f32[8,2,130,1]{2,0,3,1:T(8,128)S(1)}, f32[8,2,130,1]{2,0,3,1:T(8,128)S(1)}, u32[]{:S(2)}, u32[]{:S(2)}) collective-permute-start(f32[8,2,130,1]{2,0,3,1:T(8,128)S(1)} %copy.117), channel_id=1, source_target_pairs={{4,0},{8,4},{12,8},{16,12},{20,16},{24,20},{28,24},{5,1},{9,5},{13... | collective-permute-start | bytes 24968 | tf_op jit(solution)/shard_map/ppermute | solution.py:18
  194.7 6.1 %collective-permute-start.27 = (f32[8,2,130,1]{2,0,3,1:T(8,128)S(1)}, f32[8,2,130,1]{2,0,3,1:T(8,128)S(1)}, u32[]{:S(2)}, u32[]{:S(2)}) collective-permute-start(f32[8,2,130,1]{2,0,3,1:T(8,128)S(1)} %copy.119), channel_id=1, source_target_pairs={{0,4},{4,8},{8,12},{12,16},{16,20},{20,24},{24,28},{1,5},{5,9},{9,... | collective-permute-start | bytes 24968 | tf_op jit(solution)/shard_map/ppermute | solution.py:17
  209.9 8.0 %collective-permute-start.28 = (f32[8,2,1,256]{3,0,2,1:T(8,128)S(1)}, f32[8,2,1,256]{3,0,2,1:T(8,128)S(1)}, u32[]{:S(2)}, u32[]{:S(2)}) collective-permute-start(f32[8,2,1,256]{3,0,2,1:T(8,128)S(1)} %get-tuple-element.47), channel_id=1, source_target_pairs={{32,0},{64,32},{96,64},{128,96},{160,128},{192,160},{224,192},{33,... | collective-permute-start | bytes 49160 | tf_op jit(solution)/shard_map/ppermute | solution.py:18
  211.2 7.5 %collective-permute-start.29 = (f32[8,2,1,256]{3,0,2,1:T(8,128)S(1)}, f32[8,2,1,256]{3,0,2,1:T(8,128)S(1)}, u32[]{:S(2)}, u32[]{:S(2)}) collective-permute-start(f32[8,2,1,256]{3,0,2,1:T(8,128)S(1)} %get-tuple-element.46), channel_id=1, source_target_pairs={{0,32},{32,64},{64,96},{96,128},{128,160},{160,192},{192,224},{1,3... | collective-permute-start | bytes 49160 | tf_op jit(solution)/shard_map/ppermute | solution.py:17
  222.4 7.9 %collective-permute-start.30 = (f32[8,2,130,1]{2,0,3,1:T(8,128)S(1)}, f32[8,2,130,1]{2,0,3,1:T(8,128)S(1)}, u32[]{:S(2)}, u32[]{:S(2)}) collective-permute-start(f32[8,2,130,1]{2,0,3,1:T(8,128)S(1)} %copy.121), channel_id=1, source_target_pairs={{4,0},{8,4},{12,8},{16,12},{20,16},{24,20},{28,24},{5,1},{9,5},{13... | collective-permute-start | bytes 24968 | tf_op jit(solution)/shard_map/ppermute | solution.py:18
  240.6 7.7 %collective-permute-start.32 = (f32[8,2,1,256]{3,0,2,1:T(8,128)S(1)}, f32[8,2,1,256]{3,0,2,1:T(8,128)S(1)}, u32[]{:S(2)}, u32[]{:S(2)}) collective-permute-start(f32[8,2,1,256]{3,0,2,1:T(8,128)S(1)} %get-tuple-element.45), channel_id=1, source_target_pairs={{32,0},{64,32},{96,64},{128,96},{160,128},{192,160},{224,192},{33,... | collective-permute-start | bytes 49160 | tf_op jit(solution)/shard_map/ppermute | solution.py:18
  241.9 7.3 %collective-permute-start.33 = (f32[8,2,1,256]{3,0,2,1:T(8,128)S(1)}, f32[8,2,1,256]{3,0,2,1:T(8,128)S(1)}, u32[]{:S(2)}, u32[]{:S(2)}) collective-permute-start(f32[8,2,1,256]{3,0,2,1:T(8,128)S(1)} %get-tuple-element.44), channel_id=1, source_target_pairs={{0,32},{32,64},{64,96},{96,128},{128,160},{160,192},{192,224},{1,3... | collective-permute-start | bytes 49160 | tf_op jit(solution)/shard_map/ppermute | solution.py:17
  252.9 8.0 %collective-permute-start.34 = (f32[8,2,130,1]{2,0,3,1:T(8,128)S(1)}, f32[8,2,130,1]{2,0,3,1:T(8,128)S(1)}, u32[]{:S(2)}, u32[]{:S(2)}) collective-permute-start(f32[8,2,130,1]{2,0,3,1:T(8,128)S(1)} %copy.125), channel_id=1, source_target_pairs={{4,0},{8,4},{12,8},{16,12},{20,16},{24,20},{28,24},{5,1},{9,5},{13... | collective-permute-start | bytes 24968 | tf_op jit(solution)/shard_map/ppermute | solution.py:18
  271.3 8.0 %collective-permute-start.36 = (f32[8,2,1,256]{3,0,2,1:T(8,128)S(1)}, f32[8,2,1,256]{3,0,2,1:T(8,128)S(1)}, u32[]{:S(2)}, u32[]{:S(2)}) collective-permute-start(f32[8,2,1,256]{3,0,2,1:T(8,128)S(1)} %get-tuple-element.43), channel_id=1, source_target_pairs={{32,0},{64,32},{96,64},{128,96},{160,128},{192,160},{224,192},{33,... | collective-permute-start | bytes 49160 | tf_op jit(solution)/shard_map/ppermute | solution.py:18
  272.6 7.5 %collective-permute-start.37 = (f32[8,2,1,256]{3,0,2,1:T(8,128)S(1)}, f32[8,2,1,256]{3,0,2,1:T(8,128)S(1)}, u32[]{:S(2)}, u32[]{:S(2)}) collective-permute-start(f32[8,2,1,256]{3,0,2,1:T(8,128)S(1)} %get-tuple-element.42), channel_id=1, source_target_pairs={{0,32},{32,64},{64,96},{96,128},{128,160},{160,192},{192,224},{1,3... | collective-permute-start | bytes 49160 | tf_op jit(solution)/shard_map/ppermute | solution.py:17
  283.8 8.2 %collective-permute-start.38 = (f32[8,2,130,1]{2,0,3,1:T(8,128)S(1)}, f32[8,2,130,1]{2,0,3,1:T(8,128)S(1)}, u32[]{:S(2)}, u32[]{:S(2)}) collective-permute-start(f32[8,2,130,1]{2,0,3,1:T(8,128)S(1)} %copy.129), channel_id=1, source_target_pairs={{4,0},{8,4},{12,8},{16,12},{20,16},{24,20},{28,24},{5,1},{9,5},{13... | collective-permute-start | bytes 24968 | tf_op jit(solution)/shard_map/ppermute | solution.py:18
  302.4 8.0 %collective-permute-start.40 = (f32[8,2,1,256]{3,0,2,1:T(8,128)S(1)}, f32[8,2,1,256]{3,0,2,1:T(8,128)S(1)}, u32[]{:S(2)}, u32[]{:S(2)}) collective-permute-start(f32[8,2,1,256]{3,0,2,1:T(8,128)S(1)} %get-tuple-element.41), channel_id=1, source_target_pairs={{32,0},{64,32},{96,64},{128,96},{160,128},{192,160},{224,192},{33,... | collective-permute-start | bytes 49160 | tf_op jit(solution)/shard_map/ppermute | solution.py:18
  303.7 7.5 %collective-permute-start.41 = (f32[8,2,1,256]{3,0,2,1:T(8,128)S(1)}, f32[8,2,1,256]{3,0,2,1:T(8,128)S(1)}, u32[]{:S(2)}, u32[]{:S(2)}) collective-permute-start(f32[8,2,1,256]{3,0,2,1:T(8,128)S(1)} %get-tuple-element.40), channel_id=1, source_target_pairs={{0,32},{32,64},{64,96},{96,128},{128,160},{160,192},{192,224},{1,3... | collective-permute-start | bytes 49160 | tf_op jit(solution)/shard_map/ppermute | solution.py:17
  316.0 9.6 %collective-permute-start.42 = (f32[8,2,130,1]{2,0,3,1:T(8,128)}, f32[8,2,130,1]{2,0,3,1:T(8,128)}, u32[]{:S(2)}, u32[]{:S(2)}) collective-permute-start(f32[8,2,130,1]{2,0,3,1:T(8,128)} %copy.133), channel_id=1, source_target_pairs={{4,0},{8,4},{12,8},{16,12},{20,16},{24,20},{28,24},{5,1},{9,5},{13... | collective-permute-start | bytes 24968 | tf_op jit(solution)/shard_map/ppermute | solution.py:18
  320.4 7.6 %collective-permute-start.43 = (f32[8,2,130,1]{2,0,3,1:T(8,128)}, f32[8,2,130,1]{2,0,3,1:T(8,128)}, u32[]{:S(2)}, u32[]{:S(2)}) collective-permute-start(f32[8,2,130,1]{2,0,3,1:T(8,128)} %copy.135), channel_id=1, source_target_pairs={{0,4},{4,8},{8,12},{12,16},{16,20},{20,24},{24,28},{1,5},{5,9},{9,... | collective-permute-start | bytes 24968 | tf_op jit(solution)/shard_map/ppermute | solution.py:17
  (46 other events, 379.2 us)
Sparse Core Ops, SparseCore 0:
  338.7 89.5 all-gather.2
